TPU v7x, 512 devices: a whole 4x8x8 slice. The times are simulated.
512 devices in a mesh: dp: 64 (over x, y, z_lo), uly: 8 (over z_hi, core).
Axes of the slice: x: 4, y: 8, z: 8 (z_hi: 4, z_lo: 2; z = z_hi * 2 + z_lo), core: 2. Of those that a mesh axis runs over, the one named last changes fastest.
Arguments:
- hidden_in: bfloat16 [64, 1024, 8192], P('dp', 'uly'), may hold values from -6 to 6
- queries: bfloat16 [64, 1024, 4096], P('dp', 'uly'), may hold values from -6 to 6
- keys: bfloat16 [64, 1024, 512], P('dp', 'uly'), may hold values from -6 to 6
- values: bfloat16 [64, 1024, 512], P('dp', 'uly'), may hold values from -6 to 6
- out_grad: bfloat16 [64, 1024, 4096], P('dp', 'uly'), may hold values from -6 to 6
- doc_ids: int32 [64, 1024], P('dp', 'uly'), may hold values from 0 to 2, never falling along the last dimension, each value on 1 to 512 neighbouring positions
- flora_proj: bfloat16 [8192, 256], P('uly'), may hold values from -0.0078125 to 0.0078125
Outputs:
- flora_q: float32 [256, 4096], P('dp', 'uly')
- flora_k: float32 [256, 512], P('dp', 'uly')
- flora_v: float32 [256, 512], P('dp', 'uly')
All inputs are finite; a program needn't handle non-finite values.
Results may differ from a plain program's by a relative error of at most 0.0076.
Values may be sent and summed in bfloat16 or wider, within the bound.
No kernel may reach another device: no remote copies, remote signals or barrier semaphores. Data moves between devices by JAX's collectives and lax.ppermute only.
A program may use at most 64 MiB of HBM per device.

v0:
```python
import math

import jax
import jax.numpy as jnp
import numpy as np
from jax import lax
from jax.experimental import pallas as pl
from jax.experimental.pallas import tpu as pltpu
from jax.sharding import Mesh
from jax.sharding import PartitionSpec as P


HEAD = 128
ROWS = 128
RANK = 256
SEQ = 1024
BLOCKS = SEQ // ROWS
BAND = 640
INV_ROOT = 1.0 / math.sqrt(HEAD)
EXP2_SCALE = INV_ROOT * math.log2(math.e)
HEADS = 4
TAIL = 16
KV_AT = 2 * HEADS * ROWS
SMALL_VMEM = 16 * 2**20

NT = (((1,), (1,)), ((), ()))
TN = (((0,), (0,)), ((), ()))
NN = (((1,), (0,)), ((), ()))


def dot(a, b, dims):
    return lax.dot_general(a, b, dims, preferred_element_type=jnp.float32)


def full(shape):
    return pl.BlockSpec(shape, lambda *_: (0,) * len(shape))


SMEM = pl.BlockSpec(memory_space=pltpu.SMEM)


def pack_body(q_ref, g_ref, k_ref, v_ref, ids_ref, out_ref):
    for p in range(2):
        for h in range(HEADS):
            cols = slice((p * HEADS + h) * HEAD, (p * HEADS + h + 1) * HEAD)
            out_ref[p, h * ROWS : (h + 1) * ROWS, :] = q_ref[0, :, cols]
            out_ref[p, (HEADS + h) * ROWS : (HEADS + h + 1) * ROWS, :] = g_ref[0, :, cols]
        out_ref[p, KV_AT : KV_AT + ROWS, :] = (v_ref if p else k_ref)[0]
        out_ref[p, KV_AT + ROWS :, :] = jnp.broadcast_to(
            ids_ref[...].astype(jnp.float32), (TAIL, ROWS)
        ).astype(jnp.bfloat16)


def pack(queries, out_grad, keys, values, ids):
    wide = pl.BlockSpec((1, ROWS, 2 * HEADS * HEAD), lambda u: (0, 0, u))
    thin = pl.BlockSpec((1, ROWS, HEAD), lambda u: (0, 0, u))
    return pl.pallas_call(
        pack_body,
        grid=(4,),
        in_specs=[wide, wide, thin, thin, full((1, ROWS))],
        out_specs=pl.BlockSpec((2, KV_AT + ROWS + TAIL, HEAD), lambda u: (u, 0, 0)),
        out_shape=jax.ShapeDtypeStruct((8, KV_AT + ROWS + TAIL, HEAD), jnp.bfloat16),
        name="pack",
    )(queries, out_grad, keys, values, ids)


def attention_body(
    where_ref, all_ref, other_ref, gq_ref, gkv_ref, gk_ref, gv_ref, k_sc, v_sc, starts
):
    heads = HEADS
    i = pl.program_id(0)
    m_cols = heads * ROWS
    base = KV_AT
    core = where_ref[0]

    @pl.when(i == 0)
    def _():
        gk_ref[...] = jnp.zeros_like(gk_ref)
        gv_ref[...] = jnp.zeros_like(gv_ref)

        @pl.when(core == 0)
        def _():
            for b in range(BLOCKS):
                k_sc[b * ROWS : (b + 1) * ROWS, :] = all_ref[b, base : base + ROWS, :]
                v_sc[b * ROWS : (b + 1) * ROWS, :] = other_ref[b]

        @pl.when(core != 0)
        def _():
            for b in range(BLOCKS):
                v_sc[b * ROWS : (b + 1) * ROWS, :] = all_ref[b, base : base + ROWS, :]
                k_sc[b * ROWS : (b + 1) * ROWS, :] = other_ref[b]

        count0 = jnp.zeros((1, ROWS), jnp.float32)
        count1 = jnp.zeros((1, ROWS), jnp.float32)
        for b in range(BLOCKS):
            ids_b = all_ref[b, base + ROWS : base + ROWS + TAIL, :].astype(jnp.float32)[:1]
            count0 += jnp.where(ids_b < 0.5, 1.0, 0.0)
            count1 += jnp.where(ids_b < 1.5, 1.0, 0.0)
        starts[0] = jnp.sum(count0).astype(jnp.int32)
        starts[1] = jnp.sum(count1).astype(jnp.int32)

    start1, start2 = starts[0], starts[1]

    def start_of(pos):
        return jnp.where(pos < start1, 0, jnp.where(pos < start2, start1, start2))

    first_block = start_of(i * ROWS) // ROWS
    blocks = jnp.minimum(i - first_block + 1, BAND // ROWS)

    def step(count):
        keys = count * ROWS
        q_pos = i * ROWS + lax.broadcasted_iota(jnp.int32, (1, ROWS), 1)
        q_pos = jnp.concatenate([q_pos] * heads, axis=1)
        q_start = start_of(q_pos)
        key_start = pl.multiple_of((i - (count - 1)) * ROWS, ROWS)
        band = pl.ds(key_start, keys)
        k = k_sc[band, :]
        v = v_sc[band, :]
        q = all_ref[i, : heads * ROWS, :]
        g = all_ref[i, heads * ROWS : 2 * heads * ROWS, :]
        k_pos = key_start + lax.broadcasted_iota(jnp.int32, (keys, m_cols), 0)
        scores = dot(k, q, NT) * EXP2_SCALE
        allowed = (k_pos <= q_pos) & (k_pos >= q_start)
        scores = jnp.where(allowed, scores, -jnp.inf)
        peak = jnp.max(scores, axis=0, keepdims=True)
        weights = jnp.exp2(scores - peak)
        inv = 1.0 / jnp.sum(weights, axis=0, keepdims=True)
        grad_probs = dot(v, g, NT)
        probs = weights * inv
        delta = jnp.sum(probs * grad_probs, axis=0, keepdims=True)
        probs_low = probs.astype(jnp.bfloat16)
        grad_scores = (probs * (grad_probs - delta)).astype(jnp.bfloat16)
        gv_ref[band, :] += dot(probs_low, g, NN)
        gk_ref[band, :] += dot(grad_scores, q, NN)
        gq = (dot(k, grad_scores, TN) * INV_ROOT).astype(jnp.bfloat16)
        for h in range(heads):
            gq_ref[:, h * HEAD : (h + 1) * HEAD] = gq[:, h * ROWS : (h + 1) * ROWS].T

    for count in range(1, BAND // ROWS + 1):
        pl.when(blocks == count)(lambda count=count: step(count))

    @pl.when(i == BLOCKS - 1)
    def _():
        gkv_ref[:, :HEAD] = (gk_ref[...] * INV_ROOT).astype(jnp.bfloat16)
        gkv_ref[:, HEAD:] = gv_ref[...].astype(jnp.bfloat16)


def attention(where, everything, other):
    wide = (SEQ, HEAD)
    return pl.pallas_call(
        attention_body,
        grid=(BLOCKS,),
        in_specs=[SMEM, full(everything.shape), full(other.shape)],
        out_specs=[
            pl.BlockSpec((ROWS, HEADS * HEAD), lambda i: (i, 0)),
            full((SEQ, 2 * HEAD)),
        ],
        out_shape=[
            jax.ShapeDtypeStruct((SEQ, HEADS * HEAD), jnp.bfloat16),
            jax.ShapeDtypeStruct((SEQ, 2 * HEAD), jnp.bfloat16),
        ],
        scratch_shapes=[
            pltpu.VMEM(wide, jnp.float32),
            pltpu.VMEM(wide, jnp.float32),
            pltpu.VMEM(wide, jnp.bfloat16),
            pltpu.VMEM(wide, jnp.bfloat16),
            pltpu.SMEM((2,), jnp.int32),
        ],
        name="attention",
    )(where, everything, other)


def kernel(body, where, arrays, out_shape):
    many = isinstance(out_shape, list)
    vmem = pl.BlockSpec(memory_space=pltpu.VMEM)
    scalars = () if where is None else (where,)
    return pl.pallas_call(
        body,
        in_specs=[SMEM] * len(scalars) + [vmem] * len(arrays),
        out_specs=[vmem] * len(out_shape) if many else vmem,
        out_shape=out_shape,
        compiler_params=pltpu.CompilerParams(vmem_limit_bytes=SMALL_VMEM),
    )(*scalars, *arrays)


def project_part(side, where_ref, rows_ref, pieces, acc):
    x, y = where_ref[2], where_ref[3]
    for kx in range(4):
        part = (x - kx + 4) % 4
        for k in range(2):
            row = (y % 4) ^ (2 * k) ^ side
            at = pl.multiple_of((part * 2 + where_ref[0]) * 1024 + row * 256, 256)
            acc += dot(rows_ref[0, :, pl.ds(at, 256)], pieces[kx][k], NN)
    return acc


def near_body(where_ref, mine_ref, theirs_ref, p0, p1, p2, p3, own_ref, back_ref):
    zero = jnp.zeros((ROWS, RANK), jnp.float32)
    own_ref[...] = project_part(0, where_ref, mine_ref, (p0, p1, p2, p3), zero)
    back_ref[...] = project_part(0, where_ref, theirs_ref, (p0, p1, p2, p3), zero)


def far_body(where_ref, rows_ref, p0, p1, p2, p3, acc_ref, out_ref):
    out_ref[...] = project_part(1, where_ref, rows_ref, (p0, p1, p2, p3), acc_ref[...])


def outer_kv_body(p_ref, gkv_ref, turned_ref, send_ref):
    turned_p = p_ref[...].reshape(SEQ, RANK).T
    turned_ref[...] = turned_p
    sums = dot(turned_p, gkv_ref[...], NN).T.astype(jnp.bfloat16)
    for side in range(2):
        for u in range(8):
            at = side * HEAD + u * 16
            send_ref[u, side * 16 : (side + 1) * 16] = sums[at : at + 16]


def outer_q_body(turned_ref, gq_ref, out_ref):
    out_ref[...] = dot(turned_ref[...], gq_ref[...], NN).astype(jnp.bfloat16)


def mix_body(q_ref, kv_ref, out_ref):
    sums = [
        kv_ref[2 * g].astype(jnp.float32) + kv_ref[2 * g + 1].astype(jnp.float32)
        for g in range(4)
    ]
    stacked = jnp.concatenate(sums, axis=0).astype(jnp.bfloat16)
    row = lax.broadcasted_iota(jnp.int32, (128, 128), 0)
    col = lax.broadcasted_iota(jnp.int32, (128, 128), 1)
    head, side, c = row // 32, (row // 16) % 2, row % 16
    order = jnp.where(col == side * 64 + c * 4 + head, 1.0, 0.0).astype(jnp.bfloat16)
    sums = dot(stacked, order, TN)
    out_ref[:, :, : HEADS * HEAD] = q_ref[...].reshape(64, 4, HEADS * HEAD)
    out_ref[:, :, HEADS * HEAD :] = sums.reshape(64, 4, HEAD).astype(jnp.bfloat16)


def turned(size, by):
    return [(i, (i + by) % size) for i in range(size)]


def core_swap(x):
    return lax.ppermute(x, "c", [(0, 1), (1, 0)])


def backward(hidden_in, queries, keys, values, out_grad, doc_ids, flora_proj):
    core = lax.axis_index("c")
    zh = lax.axis_index("zh")
    x = lax.axis_index("x")
    y = lax.axis_index("y")
    where = jnp.stack([core, zh, x, y]).astype(jnp.int32)
    low = jnp.bfloat16

    rows = lax.dynamic_slice_in_dim(flora_proj, (y % 4) * 256, 256, 0)
    rows, queries, doc_ids = lax.optimization_barrier((rows, queries, doc_ids))
    rows = lax.ppermute(
        rows, ("x", "zh"), [(a * 4 + b, b * 4 + a) for a in range(4) for b in range(4)]
    )
    sent = pack(queries, out_grad, keys, values, doc_ids)
    everything = lax.all_to_all(sent, ("zh", "c"), 0, 0, tiled=True)

    def spread(piece):
        return [piece] + [lax.ppermute(piece, "x", turned(4, k)) for k in (1, 3, 2)]

    near = jnp.stack([rows, lax.ppermute(rows, "y", [(i, i ^ 2) for i in range(8)])])
    far = lax.ppermute(near, "y", [(i, i ^ 1) for i in range(8)])
    theirs = core_swap(hidden_in)
    half = jax.ShapeDtypeStruct((ROWS, RANK), jnp.float32)

    def pieces(piece):
        one, back, three, two = (*spread(piece),)
        return one, back, two, three

    near = pieces(near)
    far = pieces(far)
    own, back = kernel(near_body, where, [hidden_in, theirs, *near], [half, half])
    back = kernel(far_body, where, [theirs, *far, back], half)
    own, _ = lax.optimization_barrier((own, back))
    own = kernel(far_body, where, [hidden_in, *far, own], half)
    projected = (own + core_swap(back)).astype(low)
    other = core_swap(everything[:, KV_AT : KV_AT + ROWS, :])
    copies = jnp.broadcast_to(projected, (8, ROWS, RANK))
    all_projected = lax.all_to_all(copies, ("zh", "c"), 0, 0, tiled=True)
    where, _ = lax.optimization_barrier((where, projected))
    gq, gkv = attention(where, everything, other)
    turned_p, kv_part = kernel(
        outer_kv_body,
        None,
        [all_projected, gkv],
        [jax.ShapeDtypeStruct((RANK, SEQ), low), jax.ShapeDtypeStruct((8, 32, RANK), low)],
    )
    kv_part = lax.all_to_all(kv_part, ("zh", "c"), 0, 0, tiled=True)
    q_part = kernel(
        outer_q_body,
        None,
        [turned_p, gq],
        jax.ShapeDtypeStruct((RANK, HEADS * HEAD), low),
    )
    local = kernel(
        mix_body,
        None,
        [q_part, kv_part],
        jax.ShapeDtypeStruct((64, 4, HEADS * HEAD + HEAD), low),
    )
    parts = lax.all_to_all(local, ("x", "y", "zl"), 0, 0, tiled=True)
    sums = jnp.sum(parts.astype(jnp.float32), axis=0)
    at = HEADS * HEAD
    return sums[:, :at], sums[:, at : at + 64], sums[:, at + 64 :]


def solution(mesh):
    fine = Mesh(np.asarray(mesh.devices).reshape(4, 8, 2, 4, 2), ("x", "y", "zl", "zh", "c"))
    dp = ("x", "y", "zl")
    uly = ("zh", "c")
    placed = (P(dp, uly, None),) * 5 + (P(dp, uly), P(uly, None))
    return jax.shard_map(
        backward,
        mesh=fine,
        in_specs=placed,
        out_specs=(P(dp, uly), P(dp, uly), P(dp, uly)),
        check_vma=False,
    )
```

profile of v0, /device:TPU:1, one launch (start us, length us, event | category | flops | bytes accessed | tf_op | source)
XLA Modules:
  0.0 195.9 jit_solution(10013621323390167568)
XLA Ops:
  0.7 1.0 copy-done
  1.7 4.0 %pack.1 = bf16[8,1168,128]{2,1,0:T(8,128)(2,1)} custom-call(bf16[1,128,4096]{2,1,0:T(8,128)(2,1)} %q_ref, bf16[1,128,4096]{2,1,0:T(8,128)(2,1)} %g_ref.1, bf16[1,128,512]{2,1,0:T(8,128)(2,1)} %k_ref.1, bf16[1,128,512]{2,1,0:T(8,128)(2,1)} %v_ref.1, s32[1,128]{1,0:T(1,128)} %ids_ref), custom_call_target="tpu_custom_call" | custom-call | tf_op jit(solution)/shard_map/pack/pallas_call | solution.py:57
  5.7 11.9 %all-to-all-start.1 = ((bf16[8,1168,128]{2,1,0:T(8,128)(2,1)}), bf16[8,1168,128]{2,1,0:T(8,128)(2,1)}, u32[]{:S(2)}, u32[]{:S(2)}) async-start(bf16[8,1168,128]{2,1,0:T(8,128)(2,1)} %pack.1), calls=%async_computation.1 | async-start | bytes 4784128 | tf_op jit(solution)/shard_map/all_to_all | solution.py:258
  17.6 1.9 collective-permute-start.6
  20.2 4.2 %collective-permute-start.1 = (bf16[256,256]{1,0:T(8,128)(2,1)S(1)}, bf16[256,256]{1,0:T(8,128)(2,1)S(1)}, u32[]{:S(2)}, u32[]{:S(2)}) collective-permute-start(bf16[256,256]{1,0:T(8,128)(2,1)S(1)} %collective-permute-done), channel_id=1, source_target_pairs={{0,32},{16,48},{32,0},{48,16},{64,96},{80,112},{96,64},{112,80},{1... | collective-permute-start | bytes 393224 | tf_op jit(solution)/shard_map/ppermute | solution.py:263
  24.4 6.0 %collective-permute-done.1 = bf16[256,256]{1,0:T(8,128)(2,1)S(1)} collective-permute-done((bf16[256,256]{1,0:T(8,128)(2,1)S(1)}, bf16[256,256]{1,0:T(8,128)(2,1)S(1)}, u32[]{:S(2)}, u32[]{:S(2)}) %collective-permute-start.1) | collective-permute-done | bytes 131104 | tf_op jit(solution)/shard_map/ppermute | solution.py:263
  31.2 3.0 %collective-permute-start.2 = (bf16[2,256,256]{2,1,0:T(8,128)(2,1)}, bf16[2,256,256]{2,1,0:T(8,128)(2,1)S(1)}, u32[]{:S(2)}, u32[]{:S(2)}) collective-permute-start(bf16[2,256,256]{2,1,0:T(8,128)(2,1)} %pad_maximum_fusion.p0), channel_id=1, source_target_pairs={{0,16},{16,0},{32,48},{48,32},{64,80},{80,64},{96,112},{112,96},{1... | collective-permute-start | bytes 786440 | tf_op jit(solution)/shard_map/ppermute | solution.py:264
  34.2 63.4 %collective-permute-start.7 = (bf16[2,256,256]{2,1,0:T(8,128)(2,1)}, bf16[2,256,256]{2,1,0:T(8,128)(2,1)S(1)}, u32[]{:S(2)}, u32[]{:S(2)}) collective-permute-start(bf16[2,256,256]{2,1,0:T(8,128)(2,1)} %pad_maximum_fusion.p0), channel_id=1, source_target_pairs={{0,128},{128,256},{256,384},{384,0},{1,129},{129,257},{257,385},{3... | collective-permute-start | bytes 786440 | tf_op jit(solution)/shard_map/ppermute | solution.py:261
  97.6 2.7 %collective-permute-start.8 = (bf16[2,256,256]{2,1,0:T(8,128)(2,1)}, bf16[2,256,256]{2,1,0:T(8,128)(2,1)S(1)}, u32[]{:S(2)}, u32[]{:S(2)}) collective-permute-start(bf16[2,256,256]{2,1,0:T(8,128)(2,1)} %pad_maximum_fusion.p0), channel_id=1, source_target_pairs={{0,256},{128,384},{256,0},{384,128},{1,257},{129,385},{257,1},{385... | collective-permute-start | bytes 786440 | tf_op jit(solution)/shard_map/ppermute | solution.py:261
  100.3 3.5 %collective-permute-start.9 = (bf16[2,256,256]{2,1,0:T(8,128)(2,1)}, bf16[2,256,256]{2,1,0:T(8,128)(2,1)}, u32[]{:S(2)}, u32[]{:S(2)}) collective-permute-start(bf16[2,256,256]{2,1,0:T(8,128)(2,1)} %pad_maximum_fusion.p0), channel_id=1, source_target_pairs={{0,384},{128,0},{256,128},{384,256},{1,385},{129,1},{257,129},{385... | collective-permute-start | bytes 786440 | tf_op jit(solution)/shard_map/ppermute | solution.py:261
  103.9 1.9 collective-permute-start.3
  106.5 3.9 %collective-permute-start.4 = (bf16[2,256,256]{2,1,0:T(8,128)(2,1)S(1)}, bf16[2,256,256]{2,1,0:T(8,128)(2,1)S(1)}, u32[]{:S(2)}, u32[]{:S(2)}) collective-permute-start(bf16[2,256,256]{2,1,0:T(8,128)(2,1)S(1)} %collective-permute-done.2.p0), channel_id=1, source_target_pairs={{0,256},{128,384},{256,0},{384,128},{1,257},{129,385},{257,1},{385... | collective-permute-start | bytes 786440 | tf_op jit(solution)/shard_map/ppermute | solution.py:261
  111.2 2.6 %collective-permute-start.5 = (bf16[2,256,256]{2,1,0:T(8,128)(2,1)S(1)}, bf16[2,256,256]{2,1,0:T(8,128)(2,1)}, u32[]{:S(2)}, u32[]{:S(2)}) collective-permute-start(bf16[2,256,256]{2,1,0:T(8,128)(2,1)S(1)} %collective-permute-done.2.p0), channel_id=1, source_target_pairs={{0,384},{128,0},{256,128},{384,256},{1,385},{129,1},{257,129},{385... | collective-permute-start | bytes 786440 | tf_op jit(solution)/shard_map/ppermute | solution.py:261
  113.8 0.9 copy-done.5
  114.8 0.9 copy-done.7
  115.7 2.1 %shard_map.94 = (f32[128,256]{1,0:T(8,128)S(1)}, f32[128,256]{1,0:T(8,128)S(1)}) custom-call(s32[4]{0:T(128)S(1)} %pad_add_fusion.where_ref, bf16[1,128,8192]{2,1,0:T(8,128)(2,1)S(1)} %copy-done.1, bf16[1,128,8192]{2,1,0:T(8,128)(2,1)} %collective-permute-done.6.theirs_ref.rows_ref, bf16[2,256,256]{2,1,0:T(8,128)(2,1)} %pad_maximum_fusion.p0, ...), custom_call_target="tpu_custom_call" | custom-call | tf_op jit(solution)/shard_map/pallas_call | solution.py:177
  117.9 3.2 %collective-permute-done.4.p2 = bf16[2,256,256]{2,1,0:T(8,128)(2,1)S(1)} collective-permute-done((bf16[2,256,256]{2,1,0:T(8,128)(2,1)S(1)}, bf16[2,256,256]{2,1,0:T(8,128)(2,1)S(1)}, u32[]{:S(2)}, u32[]{:S(2)}) %collective-permute-start.4) | collective-permute-done | bytes 262176 | tf_op jit(solution)/shard_map/ppermute | solution.py:261
  121.1 1.4 collective-permute-done.5.p3
  122.5 1.9 shard_map.95
  124.4 4.0 %collective-permute-start.10 = (f32[128,256]{1,0:T(8,128)S(1)}, f32[128,256]{1,0:T(8,128)S(1)}, u32[]{:S(2)}, u32[]{:S(2)}) collective-permute-start(f32[128,256]{1,0:T(8,128)S(1)} %shard_map.95), channel_id=1, source_target_pairs={{0,1},{1,0},{2,3},{3,2},{4,5},{5,4},{6,7},{7,6},{8,9},{9,8},{10,11... | collective-permute-start | bytes 393224 | tf_op jit(solution)/shard_map/ppermute | solution.py:241
  128.5 1.3 shard_map.96
  130.6 7.4 %all-to-all-start = ((bf16[8,128,256]{2,1,0:T(8,128)(2,1)}), bf16[8,128,256]{2,1,0:T(8,128)(2,1)S(1)}, u32[]{:S(2)}, u32[]{:S(2)}) async-start(bf16[8,128,256]{2,1,0:T(8,128)(2,1)} %broadcast_in_dim.3), calls=%async_computation | async-start | bytes 1048576 | tf_op jit(solution)/shard_map/all_to_all | solution.py:281
  138.1 1.0 slice.16
  139.0 1.9 collective-permute-start.11
  141.0 1.5 collective-permute-done.11.other_ref
  143.2 10.2 %attention.1 = (bf16[1024,512]{1,0:T(8,128)(2,1)}, bf16[1024,256]{1,0:T(8,128)(2,1)}) custom-call(s32[4]{0:T(128)} %copy-done.8, bf16[8,1168,128]{2,1,0:T(8,128)(2,1)} %all-to-all-done.1.all_ref, bf16[8,128,128]{2,1,0:T(8,128)(2,1)} %copy-done.9), custom_call_target="tpu_custom_call" | custom-call | tf_op jit(solution)/shard_map/attention/pallas_call | solution.py:150
  153.5 1.0 copy-done.3
  154.5 1.1 shard_map.97
  155.6 7.2 %all-to-all-start.2 = ((bf16[8,32,256]{2,1,0:T(8,128)(2,1)}), bf16[8,32,256]{2,1,0:T(8,128)(2,1)S(1)}, u32[]{:S(2)}, u32[]{:S(2)}) async-start(bf16[8,32,256]{2,1,0:T(8,128)(2,1)} %get-tuple-element.24), calls=%async_computation.2 | async-start | bytes 262144 | tf_op jit(solution)/shard_map/all_to_all | solution.py:290
  162.8 1.2 copy-done.2
  164.4 6.3 %all-to-all-done.2.kv_ref = bf16[8,32,256]{2,1,0:T(8,128)(2,1)S(1)} async-done(((bf16[8,32,256]{2,1,0:T(8,128)(2,1)}), bf16[8,32,256]{2,1,0:T(8,128)(2,1)S(1)}, u32[]{:S(2)}, u32[]{:S(2)}) %all-to-all-start.2) | async-done | bytes 131104 | tf_op jit(solution)/shard_map/all_to_all | solution.py:290
  170.9 23.6 %all_to_all.20 = bf16[64,4,640]{2,1,0:T(4,128)(2,1)S(1)} all-to-all(bf16[64,4,640]{2,1,0:T(4,128)(2,1)S(1)} %shard_map.99), channel_id=1, replica_groups=mesh['x'=4,'y'=8,'zl'=2,'zh'=4,'c'=2] {'x','y','zl'}, dimensions={0} | all-to-all | bytes 655360 | tf_op jit(solution)/shard_map/all_to_all | solution.py:303
  (36 shorter events, 6.6 us)
Async XLA Ops:
  0.6 1.0 copy-start
  5.7 11.9 %copy-start.1 = (bf16[1,128,8192]{2,1,0:T(8,128)(2,1)S(1)}, bf16[1,128,8192]{2,1,0:T(8,128)(2,1)}, u32[]{:S(2)}) copy-start(bf16[1,128,8192]{2,1,0:T(8,128)(2,1)} %rows_ref.1) | copy-start | bytes 6291460
  5.7 124.1 %all-to-all-start.1 = ((bf16[8,1168,128]{2,1,0:T(8,128)(2,1)}), bf16[8,1168,128]{2,1,0:T(8,128)(2,1)}, u32[]{:S(2)}, u32[]{:S(2)}) async-start(bf16[8,1168,128]{2,1,0:T(8,128)(2,1)} %pack.1), calls=%async_computation.1 | async-start | bytes 4784128 | tf_op jit(solution)/shard_map/all_to_all | solution.py:258
  17.6 96.2 %collective-permute-start.6 = (bf16[1,128,8192]{2,1,0:T(8,128)(2,1)S(1)}, bf16[1,128,8192]{2,1,0:T(8,128)(2,1)}, u32[]{:S(2)}, u32[]{:S(2)}) collective-permute-start(bf16[1,128,8192]{2,1,0:T(8,128)(2,1)S(1)} %copy-done.1), channel_id=1, source_target_pairs={{0,1},{1,0},{2,3},{3,2},{4,5},{5,4},{6,7},{7,6},{8,9},{9,8},{10,11... | collective-permute-start | bytes 6291464 | tf_op jit(solution)/shard_map/ppermute | solution.py:241
  19.5 0.7 collective-permute-start
  20.2 10.3 %collective-permute-start.1 = (bf16[256,256]{1,0:T(8,128)(2,1)S(1)}, bf16[256,256]{1,0:T(8,128)(2,1)S(1)}, u32[]{:S(2)}, u32[]{:S(2)}) collective-permute-start(bf16[256,256]{1,0:T(8,128)(2,1)S(1)} %collective-permute-done), channel_id=1, source_target_pairs={{0,32},{16,48},{32,0},{48,16},{64,96},{80,112},{96,64},{112,80},{1... | collective-permute-start | bytes 393224 | tf_op jit(solution)/shard_map/ppermute | solution.py:263
  31.2 72.7 %collective-permute-start.2 = (bf16[2,256,256]{2,1,0:T(8,128)(2,1)}, bf16[2,256,256]{2,1,0:T(8,128)(2,1)S(1)}, u32[]{:S(2)}, u32[]{:S(2)}) collective-permute-start(bf16[2,256,256]{2,1,0:T(8,128)(2,1)} %pad_maximum_fusion.p0), channel_id=1, source_target_pairs={{0,16},{16,0},{32,48},{48,32},{64,80},{80,64},{96,112},{112,96},{1... | collective-permute-start | bytes 786440 | tf_op jit(solution)/shard_map/ppermute | solution.py:264
  34.2 71.5 %collective-permute-start.7 = (bf16[2,256,256]{2,1,0:T(8,128)(2,1)}, bf16[2,256,256]{2,1,0:T(8,128)(2,1)S(1)}, u32[]{:S(2)}, u32[]{:S(2)}) collective-permute-start(bf16[2,256,256]{2,1,0:T(8,128)(2,1)} %pad_maximum_fusion.p0), channel_id=1, source_target_pairs={{0,128},{128,256},{256,384},{384,0},{1,129},{129,257},{257,385},{3... | collective-permute-start | bytes 786440 | tf_op jit(solution)/shard_map/ppermute | solution.py:261
  97.6 12.8 %collective-permute-start.8 = (bf16[2,256,256]{2,1,0:T(8,128)(2,1)}, bf16[2,256,256]{2,1,0:T(8,128)(2,1)S(1)}, u32[]{:S(2)}, u32[]{:S(2)}) collective-permute-start(bf16[2,256,256]{2,1,0:T(8,128)(2,1)} %pad_maximum_fusion.p0), channel_id=1, source_target_pairs={{0,256},{128,384},{256,0},{384,128},{1,257},{129,385},{257,1},{385... | collective-permute-start | bytes 786440 | tf_op jit(solution)/shard_map/ppermute | solution.py:261
  100.3 13.5 %collective-permute-start.9 = (bf16[2,256,256]{2,1,0:T(8,128)(2,1)}, bf16[2,256,256]{2,1,0:T(8,128)(2,1)}, u32[]{:S(2)}, u32[]{:S(2)}) collective-permute-start(bf16[2,256,256]{2,1,0:T(8,128)(2,1)} %pad_maximum_fusion.p0), channel_id=1, source_target_pairs={{0,384},{128,0},{256,128},{384,256},{1,385},{129,1},{257,129},{385... | collective-permute-start | bytes 786440 | tf_op jit(solution)/shard_map/ppermute | solution.py:261
  103.9 14.0 %collective-permute-start.3 = (bf16[2,256,256]{2,1,0:T(8,128)(2,1)S(1)}, bf16[2,256,256]{2,1,0:T(8,128)(2,1)S(1)}, u32[]{:S(2)}, u32[]{:S(2)}) collective-permute-start(bf16[2,256,256]{2,1,0:T(8,128)(2,1)S(1)} %collective-permute-done.2.p0), channel_id=1, source_target_pairs={{0,128},{128,256},{256,384},{384,0},{1,129},{129,257},{257,385},{3... | collective-permute-start | bytes 786440 | tf_op jit(solution)/shard_map/ppermute | solution.py:261
  105.8 0.7 copy-start.4
  106.5 14.6 %collective-permute-start.4 = (bf16[2,256,256]{2,1,0:T(8,128)(2,1)S(1)}, bf16[2,256,256]{2,1,0:T(8,128)(2,1)S(1)}, u32[]{:S(2)}, u32[]{:S(2)}) collective-permute-start(bf16[2,256,256]{2,1,0:T(8,128)(2,1)S(1)} %collective-permute-done.2.p0), channel_id=1, source_target_pairs={{0,256},{128,384},{256,0},{384,128},{1,257},{129,385},{257,1},{385... | collective-permute-start | bytes 786440 | tf_op jit(solution)/shard_map/ppermute | solution.py:261
  110.4 0.7 copy-start.6
  111.2 11.3 %collective-permute-start.5 = (bf16[2,256,256]{2,1,0:T(8,128)(2,1)S(1)}, bf16[2,256,256]{2,1,0:T(8,128)(2,1)}, u32[]{:S(2)}, u32[]{:S(2)}) collective-permute-start(bf16[2,256,256]{2,1,0:T(8,128)(2,1)S(1)} %collective-permute-done.2.p0), channel_id=1, source_target_pairs={{0,384},{128,0},{256,128},{384,256},{1,385},{129,1},{257,129},{385... | collective-permute-start | bytes 786440 | tf_op jit(solution)/shard_map/ppermute | solution.py:261
  113.8 14.6 %copy-start.8 = (s32[4]{0:T(128)}, s32[4]{0:T(128)S(1)}, u32[]{:S(2)}) copy-start(s32[4]{0:T(128)S(1)} %pad_add_fusion.where_ref) | copy-start | bytes 52
  113.8 1.0 copy-start.5
  114.8 0.9 copy-start.7
  124.4 5.3 %collective-permute-start.10 = (f32[128,256]{1,0:T(8,128)S(1)}, f32[128,256]{1,0:T(8,128)S(1)}, u32[]{:S(2)}, u32[]{:S(2)}) collective-permute-start(f32[128,256]{1,0:T(8,128)S(1)} %shard_map.95), channel_id=1, source_target_pairs={{0,1},{1,0},{2,3},{3,2},{4,5},{5,4},{6,7},{7,6},{8,9},{9,8},{10,11... | collective-permute-start | bytes 393224 | tf_op jit(solution)/shard_map/ppermute | solution.py:241
  130.6 22.8 %all-to-all-start = ((bf16[8,128,256]{2,1,0:T(8,128)(2,1)}), bf16[8,128,256]{2,1,0:T(8,128)(2,1)S(1)}, u32[]{:S(2)}, u32[]{:S(2)}) async-start(bf16[8,128,256]{2,1,0:T(8,128)(2,1)} %broadcast_in_dim.3), calls=%async_computation | async-start | bytes 1048576 | tf_op jit(solution)/shard_map/all_to_all | solution.py:281
  139.0 3.4 %collective-permute-start.11 = (bf16[8,128,128]{2,1,0:T(8,128)(2,1)S(1)}, bf16[8,128,128]{2,1,0:T(8,128)(2,1)S(1)}, u32[]{:S(2)}, u32[]{:S(2)}) collective-permute-start(bf16[8,128,128]{2,1,0:T(8,128)(2,1)S(1)} %slice.16), channel_id=1, source_target_pairs={{0,1},{1,0},{2,3},{3,2},{4,5},{5,4},{6,7},{7,6},{8,9},{9,8},{10,11... | collective-permute-start | bytes 786440 | tf_op jit(solution)/shard_map/ppermute | solution.py:241
  142.5 0.7 copy-start.9
  153.5 1.0 copy-start.3
  155.6 15.2 %all-to-all-start.2 = ((bf16[8,32,256]{2,1,0:T(8,128)(2,1)}), bf16[8,32,256]{2,1,0:T(8,128)(2,1)S(1)}, u32[]{:S(2)}, u32[]{:S(2)}) async-start(bf16[8,32,256]{2,1,0:T(8,128)(2,1)} %get-tuple-element.24), calls=%async_computation.2 | async-start | bytes 262144 | tf_op jit(solution)/shard_map/all_to_all | solution.py:290
  162.8 1.2 copy-start.2
where the time goes:
time: 198 us; the launch traced here: 196 us
  starting transfers between devices  120 us (61%)
  blocking collectives  23.6 us (12%)
  Pallas kernels  21.3 us (11%)
  waiting for transfers between devices  18.5 us (9%)
  local copies, waits for them, and re-layouts  10.4 us (5%)
    ppermute x6, starting transfers between devices, spread(): return [piece] + [lax.ppermute(piece, 'x', turned(4, k)) for k in (1, 3, 2)]  78 us
    all_to_all x1, blocking collectives, backward(): parts = lax.all_to_all(local, ('x', 'y', 'zl'), 0, 0, tiled=True)  23.6 us
    all_to_all x1, starting transfers between devices, backward(): everything = lax.all_to_all(sent, ('zh', 'c'), 0, 0, tiled=True)  11.9 us
    pallas_call x1, Pallas kernels, attention(): pl.pallas_call(attention_body, grid=(BLOCKS,), in_specs=[SMEM, full(every...  10.2 us
    ppermute x3, starting transfers between devices, core_swap(): return lax.ppermute(x, 'c', [(0, 1), (1, 0)])  7.88 us
    all_to_all x1, starting transfers between devices, backward(): all_projected = lax.all_to_all(copies, ('zh', 'c'), 0, 0, tiled=True)  7.44 us
    unnamed x20, local copies, waits for them, and re-layouts  7.34 us
    all_to_all x1, starting transfers between devices, backward(): kv_part = lax.all_to_all(kv_part, ('zh', 'c'), 0, 0, tiled=True)  7.19 us
  transfers between devices with their start and end apart: 15, of which 5 were waited for; matrix products, arithmetic and copies ran while one was open for 1% of the time, Pallas kernels for 8%

commit v1 on v0

--- a/solution.py
+++ b/solution.py
@@ -22,6 +22,7 @@
 TAIL = 16
 KV_AT = 2 * HEADS * ROWS
 SMALL_VMEM = 16 * 2**20
+PEERS_AT_ONCE = 2
 
 NT = (((1,), (1,)), ((), ()))
 TN = (((0,), (0,)), ((), ()))
@@ -40,25 +41,26 @@
 
 
 def pack_body(q_ref, g_ref, k_ref, v_ref, ids_ref, out_ref):
-    for p in range(2):
+    ids = jnp.broadcast_to(ids_ref[...].astype(jnp.float32), (TAIL, ROWS)).astype(jnp.bfloat16)
+    for p in range(PEERS_AT_ONCE):
         for h in range(HEADS):
             cols = slice((p * HEADS + h) * HEAD, (p * HEADS + h + 1) * HEAD)
             out_ref[p, h * ROWS : (h + 1) * ROWS, :] = q_ref[0, :, cols]
             out_ref[p, (HEADS + h) * ROWS : (HEADS + h + 1) * ROWS, :] = g_ref[0, :, cols]
-        out_ref[p, KV_AT : KV_AT + ROWS, :] = (v_ref if p else k_ref)[0]
-        out_ref[p, KV_AT + ROWS :, :] = jnp.broadcast_to(
-            ids_ref[...].astype(jnp.float32), (TAIL, ROWS)
-        ).astype(jnp.bfloat16)
+        cols = slice((p // 2) * HEAD, (p // 2 + 1) * HEAD)
+        out_ref[p, KV_AT : KV_AT + ROWS, :] = (v_ref if p % 2 else k_ref)[0, :, cols]
+        out_ref[p, KV_AT + ROWS :, :] = ids
 
 
 def pack(queries, out_grad, keys, values, ids):
-    wide = pl.BlockSpec((1, ROWS, 2 * HEADS * HEAD), lambda u: (0, 0, u))
-    thin = pl.BlockSpec((1, ROWS, HEAD), lambda u: (0, 0, u))
+    n = PEERS_AT_ONCE
+    wide = pl.BlockSpec((1, ROWS, n * HEADS * HEAD), lambda u: (0, 0, u))
+    thin = pl.BlockSpec((1, ROWS, n // 2 * HEAD), lambda u: (0, 0, u))
     return pl.pallas_call(
         pack_body,
-        grid=(4,),
+        grid=(8 // n,),
         in_specs=[wide, wide, thin, thin, full((1, ROWS))],
-        out_specs=pl.BlockSpec((2, KV_AT + ROWS + TAIL, HEAD), lambda u: (u, 0, 0)),
+        out_specs=pl.BlockSpec((n, KV_AT + ROWS + TAIL, HEAD), lambda u: (u, 0, 0)),
         out_shape=jax.ShapeDtypeStruct((8, KV_AT + ROWS + TAIL, HEAD), jnp.bfloat16),
         name="pack",
     )(queries, out_grad, keys, values, ids)
@@ -204,6 +206,12 @@
     out_ref[...] = project_part(1, where_ref, rows_ref, (p0, p1, p2, p3), acc_ref[...])
 
 
+def finish_body(own_ref, got_ref, out_ref):
+    projected = (own_ref[...] + got_ref[...]).astype(jnp.bfloat16)
+    for u in range(8):
+        out_ref[u] = projected
+
+
 def outer_kv_body(p_ref, gkv_ref, turned_ref, send_ref):
     turned_p = p_ref[...].reshape(SEQ, RANK).T
     turned_ref[...] = turned_p
@@ -275,11 +283,15 @@
     back = kernel(far_body, where, [theirs, *far, back], half)
     own, _ = lax.optimization_barrier((own, back))
     own = kernel(far_body, where, [hidden_in, *far, own], half)
-    projected = (own + core_swap(back)).astype(low)
+    copies = kernel(
+        finish_body,
+        None,
+        [own, core_swap(back)],
+        jax.ShapeDtypeStruct((8, ROWS, RANK), low),
+    )
     other = core_swap(everything[:, KV_AT : KV_AT + ROWS, :])
-    copies = jnp.broadcast_to(projected, (8, ROWS, RANK))
     all_projected = lax.all_to_all(copies, ("zh", "c"), 0, 0, tiled=True)
-    where, _ = lax.optimization_barrier((where, projected))
+    where, _ = lax.optimization_barrier((where, copies))
     gq, gkv = attention(where, everything, other)
     turned_p, kv_part = kernel(
         outer_kv_body,
@@ -301,9 +313,16 @@
         jax.ShapeDtypeStruct((64, 4, HEADS * HEAD + HEAD), low),
     )
     parts = lax.all_to_all(local, ("x", "y", "zl"), 0, 0, tiled=True)
-    sums = jnp.sum(parts.astype(jnp.float32), axis=0)
     at = HEADS * HEAD
-    return sums[:, :at], sums[:, at : at + 64], sums[:, at + 64 :]
+
+    def summed(columns):
+        return jnp.sum(columns.astype(jnp.float32), axis=0)
+
+    return (
+        summed(parts[:, :, :at]),
+        summed(parts[:, :, at : at + 64]),
+        summed(parts[:, :, at + 64 :]),
+    )
 
 
 def solution(mesh):

time: 198 us -> 198 us (level)
  local copies, waits for them, and re-layouts: 10.4 us -> 8.29 us
  blocking collectives: 23.6 us -> 21.5 us
    all_to_all x1, blocking collectives: 23.6 us -> 21.5 us  [backward(): parts = lax.all_to_all(local, ('x', 'y', 'zl'), 0, 0, tiled=True)]
    pallas_call x6 -> x7, Pallas kernels: 7.04 us -> 7.89 us  [kernel(): pl.pallas_call(body, in_specs=[SMEM] * len(scalars) + [vmem] * len(arrays...]
  transfers between devices with their start and end apart: 15 -> 15, of which waited for: 5 -> 5; matrix products, arithmetic and copies ran while one was open for 1% -> 1% of each run, Pallas kernels for 8% -> 9%
where the time goes in v1:
time: 198 us; the launch traced here: 196 us
  starting transfers between devices  121 us (61%)
  Pallas kernels  22.1 us (11%)
  blocking collectives  21.5 us (11%)
  waiting for transfers between devices  20.4 us (10%)
  local copies, waits for them, and re-layouts  8.29 us (4%)
  other arithmetic  2.29 us (1%)
    ppermute x6, starting transfers between devices, spread(): return [piece] + [lax.ppermute(piece, 'x', turned(4, k)) for k in (1, 3, 2)]  77.9 us
    all_to_all x1, blocking collectives, backward(): parts = lax.all_to_all(local, ('x', 'y', 'zl'), 0, 0, tiled=True)  21.5 us
    all_to_all x1, starting transfers between devices, backward(): everything = lax.all_to_all(sent, ('zh', 'c'), 0, 0, tiled=True)  11.9 us
    pallas_call x1, Pallas kernels, attention(): pl.pallas_call(attention_body, grid=(BLOCKS,), in_specs=[SMEM, full(every...  10.2 us
    ppermute x3, starting transfers between devices, core_swap(): return lax.ppermute(x, 'c', [(0, 1), (1, 0)])  8.63 us
    pallas_call x7, Pallas kernels, kernel(): pl.pallas_call(body, in_specs=[SMEM] * len(scalars) + [vmem] * len(arrays...  7.89 us
    unnamed x20, local copies, waits for them, and re-layouts  7.31 us
    all_to_all x1, starting transfers between devices, backward(): kv_part = lax.all_to_all(kv_part, ('zh', 'c'), 0, 0, tiled=True)  7.19 us
  transfers between devices with their start and end apart: 15, of which 5 were waited for; matrix products, arithmetic and copies ran while one was open for 1% of the time, Pallas kernels for 9%

profile of v1, /device:TPU:1, one launch (start us, length us, event | category | flops | bytes accessed | tf_op | source)
XLA Modules:
  0.0 196.2 jit_solution(14041851658388279599)
XLA Ops:
  0.7 1.0 copy-done
  1.7 4.0 %pack.1 = bf16[8,1168,128]{2,1,0:T(8,128)(2,1)} custom-call(bf16[1,128,4096]{2,1,0:T(8,128)(2,1)} %q_ref, bf16[1,128,4096]{2,1,0:T(8,128)(2,1)} %g_ref.1, bf16[1,128,512]{2,1,0:T(8,128)(2,1)} %k_ref.1, bf16[1,128,512]{2,1,0:T(8,128)(2,1)} %v_ref.1, s32[1,128]{1,0:T(1,128)} %ids_ref), custom_call_target="tpu_custom_call" | custom-call | tf_op jit(solution)/shard_map/pack/pallas_call | solution.py:59
  5.7 11.9 %all-to-all-start.1 = ((bf16[8,1168,128]{2,1,0:T(8,128)(2,1)}), bf16[8,1168,128]{2,1,0:T(8,128)(2,1)}, u32[]{:S(2)}, u32[]{:S(2)}) async-start(bf16[8,1168,128]{2,1,0:T(8,128)(2,1)} %pack.1), calls=%async_computation.1 | async-start | bytes 4784128 | tf_op jit(solution)/shard_map/all_to_all | solution.py:266
  17.6 1.9 collective-permute-start.6
  20.2 4.2 %collective-permute-start.1 = (bf16[256,256]{1,0:T(8,128)(2,1)S(1)}, bf16[256,256]{1,0:T(8,128)(2,1)S(1)}, u32[]{:S(2)}, u32[]{:S(2)}) collective-permute-start(bf16[256,256]{1,0:T(8,128)(2,1)S(1)} %collective-permute-done), channel_id=1, source_target_pairs={{0,32},{16,48},{32,0},{48,16},{64,96},{80,112},{96,64},{112,80},{1... | collective-permute-start | bytes 393224 | tf_op jit(solution)/shard_map/ppermute | solution.py:271
  24.4 6.0 %collective-permute-done.1 = bf16[256,256]{1,0:T(8,128)(2,1)S(1)} collective-permute-done((bf16[256,256]{1,0:T(8,128)(2,1)S(1)}, bf16[256,256]{1,0:T(8,128)(2,1)S(1)}, u32[]{:S(2)}, u32[]{:S(2)}) %collective-permute-start.1) | collective-permute-done | bytes 131104 | tf_op jit(solution)/shard_map/ppermute | solution.py:271
  31.2 3.0 %collective-permute-start.2 = (bf16[2,256,256]{2,1,0:T(8,128)(2,1)}, bf16[2,256,256]{2,1,0:T(8,128)(2,1)S(1)}, u32[]{:S(2)}, u32[]{:S(2)}) collective-permute-start(bf16[2,256,256]{2,1,0:T(8,128)(2,1)} %pad_maximum_fusion.p0), channel_id=1, source_target_pairs={{0,16},{16,0},{32,48},{48,32},{64,80},{80,64},{96,112},{112,96},{1... | collective-permute-start | bytes 786440 | tf_op jit(solution)/shard_map/ppermute | solution.py:272
  34.3 63.0 %collective-permute-start.9 = (bf16[2,256,256]{2,1,0:T(8,128)(2,1)}, bf16[2,256,256]{2,1,0:T(8,128)(2,1)S(1)}, u32[]{:S(2)}, u32[]{:S(2)}) collective-permute-start(bf16[2,256,256]{2,1,0:T(8,128)(2,1)} %pad_maximum_fusion.p0), channel_id=1, source_target_pairs={{0,384},{128,0},{256,128},{384,256},{1,385},{129,1},{257,129},{385... | collective-permute-start | bytes 786440 | tf_op jit(solution)/shard_map/ppermute | solution.py:269
  97.2 4.1 %collective-permute-start.8 = (bf16[2,256,256]{2,1,0:T(8,128)(2,1)}, bf16[2,256,256]{2,1,0:T(8,128)(2,1)S(1)}, u32[]{:S(2)}, u32[]{:S(2)}) collective-permute-start(bf16[2,256,256]{2,1,0:T(8,128)(2,1)} %pad_maximum_fusion.p0), channel_id=1, source_target_pairs={{0,256},{128,384},{256,0},{384,128},{1,257},{129,385},{257,1},{385... | collective-permute-start | bytes 786440 | tf_op jit(solution)/shard_map/ppermute | solution.py:269
  101.3 1.9 collective-permute-start.7
  103.3 4.6 %collective-permute-start.5 = (bf16[2,256,256]{2,1,0:T(8,128)(2,1)S(1)}, bf16[2,256,256]{2,1,0:T(8,128)(2,1)S(1)}, u32[]{:S(2)}, u32[]{:S(2)}) collective-permute-start(bf16[2,256,256]{2,1,0:T(8,128)(2,1)S(1)} %collective-permute-done.2.p0), channel_id=1, source_target_pairs={{0,384},{128,0},{256,128},{384,256},{1,385},{129,1},{257,129},{385... | collective-permute-start | bytes 786440 | tf_op jit(solution)/shard_map/ppermute | solution.py:269
  108.6 1.9 collective-permute-start.4
  111.2 2.5 %collective-permute-start.3 = (bf16[2,256,256]{2,1,0:T(8,128)(2,1)S(1)}, bf16[2,256,256]{2,1,0:T(8,128)(2,1)}, u32[]{:S(2)}, u32[]{:S(2)}) collective-permute-start(bf16[2,256,256]{2,1,0:T(8,128)(2,1)S(1)} %collective-permute-done.2.p0), channel_id=1, source_target_pairs={{0,128},{128,256},{256,384},{384,0},{1,129},{129,257},{257,385},{3... | collective-permute-start | bytes 786440 | tf_op jit(solution)/shard_map/ppermute | solution.py:269
  114.2 0.9 copy-done.5
  115.1 0.9 copy-done.7
  116.1 2.2 %shard_map.94 = (f32[128,256]{1,0:T(8,128)S(1)}, f32[128,256]{1,0:T(8,128)S(1)}) custom-call(s32[4]{0:T(128)S(1)} %pad_add_fusion.where_ref, bf16[1,128,8192]{2,1,0:T(8,128)(2,1)S(1)} %copy-done.1, bf16[1,128,8192]{2,1,0:T(8,128)(2,1)} %collective-permute-done.6.theirs_ref.rows_ref, bf16[2,256,256]{2,1,0:T(8,128)(2,1)} %pad_maximum_fusion.p0, ...), custom_call_target="tpu_custom_call" | custom-call | tf_op jit(solution)/shard_map/pallas_call | solution.py:179
  118.3 5.4 %collective-permute-done.3.p1 = bf16[2,256,256]{2,1,0:T(8,128)(2,1)} collective-permute-done((bf16[2,256,256]{2,1,0:T(8,128)(2,1)S(1)}, bf16[2,256,256]{2,1,0:T(8,128)(2,1)}, u32[]{:S(2)}, u32[]{:S(2)}) %collective-permute-start.3) | collective-permute-done | bytes 262176 | tf_op jit(solution)/shard_map/ppermute | solution.py:269
  123.7 1.9 shard_map.95
  125.6 4.8 %collective-permute-start.10 = (f32[128,256]{1,0:T(8,128)S(1)}, f32[128,256]{1,0:T(8,128)S(1)}, u32[]{:S(2)}, u32[]{:S(2)}) collective-permute-start(f32[128,256]{1,0:T(8,128)S(1)} %shard_map.95), channel_id=1, source_target_pairs={{0,1},{1,0},{2,3},{3,2},{4,5},{5,4},{6,7},{7,6},{8,9},{9,8},{10,11... | collective-permute-start | bytes 393224 | tf_op jit(solution)/shard_map/ppermute | solution.py:249
  130.4 1.3 shard_map.96.own_ref
  131.7 0.8 shard_map.97
  132.5 7.1 %all-to-all-start = ((bf16[8,128,256]{2,1,0:T(8,128)(2,1)}), bf16[8,128,256]{2,1,0:T(8,128)(2,1)S(1)}, u32[]{:S(2)}, u32[]{:S(2)}) async-start(bf16[8,128,256]{2,1,0:T(8,128)(2,1)} %shard_map.97), calls=%async_computation | async-start | bytes 1048576 | tf_op jit(solution)/shard_map/all_to_all | solution.py:293
  139.6 1.0 slice.16
  140.6 1.9 collective-permute-start.11
  142.5 1.5 collective-permute-done.11.other_ref
  144.7 10.2 %attention.1 = (bf16[1024,512]{1,0:T(8,128)(2,1)}, bf16[1024,256]{1,0:T(8,128)(2,1)}) custom-call(s32[4]{0:T(128)} %copy-done.8, bf16[8,1168,128]{2,1,0:T(8,128)(2,1)} %all-to-all-done.1.all_ref, bf16[8,128,128]{2,1,0:T(8,128)(2,1)} %copy-done.9), custom_call_target="tpu_custom_call" | custom-call | tf_op jit(solution)/shard_map/attention/pallas_call | solution.py:152
  155.0 1.0 copy-done.3
  156.0 1.1 shard_map.98
  157.1 7.2 %all-to-all-start.2 = ((bf16[8,32,256]{2,1,0:T(8,128)(2,1)}), bf16[8,32,256]{2,1,0:T(8,128)(2,1)S(1)}, u32[]{:S(2)}, u32[]{:S(2)}) async-start(bf16[8,32,256]{2,1,0:T(8,128)(2,1)} %get-tuple-element.24), calls=%async_computation.2 | async-start | bytes 262144 | tf_op jit(solution)/shard_map/all_to_all | solution.py:302
  164.3 1.2 copy-done.2
  165.9 7.0 %all-to-all-done.2.kv_ref = bf16[8,32,256]{2,1,0:T(8,128)(2,1)S(1)} async-done(((bf16[8,32,256]{2,1,0:T(8,128)(2,1)}), bf16[8,32,256]{2,1,0:T(8,128)(2,1)S(1)}, u32[]{:S(2)}, u32[]{:S(2)}) %all-to-all-start.2) | async-done | bytes 131104 | tf_op jit(solution)/shard_map/all_to_all | solution.py:302
  173.2 21.5 %all_to_all.20 = bf16[64,4,640]{2,1,0:T(4,128)(2,1)S(1)} all-to-all(bf16[64,4,640]{2,1,0:T(4,128)(2,1)S(1)} %shard_map.100), channel_id=1, replica_groups=mesh['x'=4,'y'=8,'zl'=2,'zh'=4,'c'=2] {'x','y','zl'}, dimensions={0} | all-to-all | bytes 655360 | tf_op jit(solution)/shard_map/all_to_all | solution.py:315
  (34 shorter events, 6.1 us)
Async XLA Ops:
  0.6 1.0 copy-start
  5.7 11.9 %copy-start.1 = (bf16[1,128,8192]{2,1,0:T(8,128)(2,1)S(1)}, bf16[1,128,8192]{2,1,0:T(8,128)(2,1)}, u32[]{:S(2)}) copy-start(bf16[1,128,8192]{2,1,0:T(8,128)(2,1)} %rows_ref.1) | copy-start | bytes 6291460
  5.7 126.9 %all-to-all-start.1 = ((bf16[8,1168,128]{2,1,0:T(8,128)(2,1)}), bf16[8,1168,128]{2,1,0:T(8,128)(2,1)}, u32[]{:S(2)}, u32[]{:S(2)}) async-start(bf16[8,1168,128]{2,1,0:T(8,128)(2,1)} %pack.1), calls=%async_computation.1 | async-start | bytes 4784128 | tf_op jit(solution)/shard_map/all_to_all | solution.py:266
  17.6 96.6 %collective-permute-start.6 = (bf16[1,128,8192]{2,1,0:T(8,128)(2,1)S(1)}, bf16[1,128,8192]{2,1,0:T(8,128)(2,1)}, u32[]{:S(2)}, u32[]{:S(2)}) collective-permute-start(bf16[1,128,8192]{2,1,0:T(8,128)(2,1)S(1)} %copy-done.1), channel_id=1, source_target_pairs={{0,1},{1,0},{2,3},{3,2},{4,5},{5,4},{6,7},{7,6},{8,9},{9,8},{10,11... | collective-permute-start | bytes 6291464 | tf_op jit(solution)/shard_map/ppermute | solution.py:249
  19.5 0.7 collective-permute-start
  20.2 10.3 %collective-permute-start.1 = (bf16[256,256]{1,0:T(8,128)(2,1)S(1)}, bf16[256,256]{1,0:T(8,128)(2,1)S(1)}, u32[]{:S(2)}, u32[]{:S(2)}) collective-permute-start(bf16[256,256]{1,0:T(8,128)(2,1)S(1)} %collective-permute-done), channel_id=1, source_target_pairs={{0,32},{16,48},{32,0},{48,16},{64,96},{80,112},{96,64},{112,80},{1... | collective-permute-start | bytes 393224 | tf_op jit(solution)/shard_map/ppermute | solution.py:271
  31.2 72.1 %collective-permute-start.2 = (bf16[2,256,256]{2,1,0:T(8,128)(2,1)}, bf16[2,256,256]{2,1,0:T(8,128)(2,1)S(1)}, u32[]{:S(2)}, u32[]{:S(2)}) collective-permute-start(bf16[2,256,256]{2,1,0:T(8,128)(2,1)} %pad_maximum_fusion.p0), channel_id=1, source_target_pairs={{0,16},{16,0},{32,48},{48,32},{64,80},{80,64},{96,112},{112,96},{1... | collective-permute-start | bytes 786440 | tf_op jit(solution)/shard_map/ppermute | solution.py:272
  34.3 73.6 %collective-permute-start.9 = (bf16[2,256,256]{2,1,0:T(8,128)(2,1)}, bf16[2,256,256]{2,1,0:T(8,128)(2,1)S(1)}, u32[]{:S(2)}, u32[]{:S(2)}) collective-permute-start(bf16[2,256,256]{2,1,0:T(8,128)(2,1)} %pad_maximum_fusion.p0), channel_id=1, source_target_pairs={{0,384},{128,0},{256,128},{384,256},{1,385},{129,1},{257,129},{385... | collective-permute-start | bytes 786440 | tf_op jit(solution)/shard_map/ppermute | solution.py:269
  97.2 13.3 %collective-permute-start.8 = (bf16[2,256,256]{2,1,0:T(8,128)(2,1)}, bf16[2,256,256]{2,1,0:T(8,128)(2,1)S(1)}, u32[]{:S(2)}, u32[]{:S(2)}) collective-permute-start(bf16[2,256,256]{2,1,0:T(8,128)(2,1)} %pad_maximum_fusion.p0), channel_id=1, source_target_pairs={{0,256},{128,384},{256,0},{384,128},{1,257},{129,385},{257,1},{385... | collective-permute-start | bytes 786440 | tf_op jit(solution)/shard_map/ppermute | solution.py:269
  101.3 12.8 %collective-permute-start.7 = (bf16[2,256,256]{2,1,0:T(8,128)(2,1)}, bf16[2,256,256]{2,1,0:T(8,128)(2,1)}, u32[]{:S(2)}, u32[]{:S(2)}) collective-permute-start(bf16[2,256,256]{2,1,0:T(8,128)(2,1)} %pad_maximum_fusion.p0), channel_id=1, source_target_pairs={{0,128},{128,256},{256,384},{384,0},{1,129},{129,257},{257,385},{3... | collective-permute-start | bytes 786440 | tf_op jit(solution)/shard_map/ppermute | solution.py:269
  103.3 15.0 %collective-permute-start.5 = (bf16[2,256,256]{2,1,0:T(8,128)(2,1)S(1)}, bf16[2,256,256]{2,1,0:T(8,128)(2,1)S(1)}, u32[]{:S(2)}, u32[]{:S(2)}) collective-permute-start(bf16[2,256,256]{2,1,0:T(8,128)(2,1)S(1)} %collective-permute-done.2.p0), channel_id=1, source_target_pairs={{0,384},{128,0},{256,128},{384,256},{1,385},{129,1},{257,129},{385... | collective-permute-start | bytes 786440 | tf_op jit(solution)/shard_map/ppermute | solution.py:269
  107.9 0.7 copy-start.4
  108.6 9.6 %collective-permute-start.4 = (bf16[2,256,256]{2,1,0:T(8,128)(2,1)S(1)}, bf16[2,256,256]{2,1,0:T(8,128)(2,1)S(1)}, u32[]{:S(2)}, u32[]{:S(2)}) collective-permute-start(bf16[2,256,256]{2,1,0:T(8,128)(2,1)S(1)} %collective-permute-done.2.p0), channel_id=1, source_target_pairs={{0,256},{128,384},{256,0},{384,128},{1,257},{129,385},{257,1},{385... | collective-permute-start | bytes 786440 | tf_op jit(solution)/shard_map/ppermute | solution.py:269
  110.5 0.7 copy-start.6
  111.2 12.4 %collective-permute-start.3 = (bf16[2,256,256]{2,1,0:T(8,128)(2,1)S(1)}, bf16[2,256,256]{2,1,0:T(8,128)(2,1)}, u32[]{:S(2)}, u32[]{:S(2)}) collective-permute-start(bf16[2,256,256]{2,1,0:T(8,128)(2,1)S(1)} %collective-permute-done.2.p0), channel_id=1, source_target_pairs={{0,128},{128,256},{256,384},{384,0},{1,129},{129,257},{257,385},{3... | collective-permute-start | bytes 786440 | tf_op jit(solution)/shard_map/ppermute | solution.py:269
  113.8 16.6 %copy-start.8 = (s32[4]{0:T(128)}, s32[4]{0:T(128)S(1)}, u32[]{:S(2)}) copy-start(s32[4]{0:T(128)S(1)} %pad_add_fusion.where_ref) | copy-start | bytes 52
  114.2 1.0 copy-start.5
  115.1 0.9 copy-start.7
  125.6 6.1 %collective-permute-start.10 = (f32[128,256]{1,0:T(8,128)S(1)}, f32[128,256]{1,0:T(8,128)S(1)}, u32[]{:S(2)}, u32[]{:S(2)}) collective-permute-start(f32[128,256]{1,0:T(8,128)S(1)} %shard_map.95), channel_id=1, source_target_pairs={{0,1},{1,0},{2,3},{3,2},{4,5},{5,4},{6,7},{7,6},{8,9},{9,8},{10,11... | collective-permute-start | bytes 393224 | tf_op jit(solution)/shard_map/ppermute | solution.py:249
  132.5 22.5 %all-to-all-start = ((bf16[8,128,256]{2,1,0:T(8,128)(2,1)}), bf16[8,128,256]{2,1,0:T(8,128)(2,1)S(1)}, u32[]{:S(2)}, u32[]{:S(2)}) async-start(bf16[8,128,256]{2,1,0:T(8,128)(2,1)} %shard_map.97), calls=%async_computation | async-start | bytes 1048576 | tf_op jit(solution)/shard_map/all_to_all | solution.py:293
  140.6 3.4 %collective-permute-start.11 = (bf16[8,128,128]{2,1,0:T(8,128)(2,1)S(1)}, bf16[8,128,128]{2,1,0:T(8,128)(2,1)S(1)}, u32[]{:S(2)}, u32[]{:S(2)}) collective-permute-start(bf16[8,128,128]{2,1,0:T(8,128)(2,1)S(1)} %slice.16), channel_id=1, source_target_pairs={{0,1},{1,0},{2,3},{3,2},{4,5},{5,4},{6,7},{7,6},{8,9},{9,8},{10,11... | collective-permute-start | bytes 786440 | tf_op jit(solution)/shard_map/ppermute | solution.py:249
  144.0 0.7 copy-start.9
  155.0 1.0 copy-start.3
  157.1 15.9 %all-to-all-start.2 = ((bf16[8,32,256]{2,1,0:T(8,128)(2,1)}), bf16[8,32,256]{2,1,0:T(8,128)(2,1)S(1)}, u32[]{:S(2)}, u32[]{:S(2)}) async-start(bf16[8,32,256]{2,1,0:T(8,128)(2,1)} %get-tuple-element.24), calls=%async_computation.2 | async-start | bytes 262144 | tf_op jit(solution)/shard_map/all_to_all | solution.py:302
  164.3 1.2 copy-start.2
